TPU v7x, 32 devices: a whole 2x2x4 slice. The times are simulated.
32 devices in a mesh: section: 8 (over y, x, core), shard: 4 (over z).
Axes of the slice: x: 2, y: 2, z: 4, core: 2. Of those that a mesh axis runs over, the one named last changes fastest.
Arguments:
- kept_slab: bfloat16 [131072, 768], P(('section', 'shard')), may hold values from -1 to 1, as said below
- new_rows: bfloat16 [4, 256, 768], P(None, ('section', 'shard')), may hold values from -1 to 1, as said below
- append_mask: int32 [4, 256], P(None, ('section', 'shard')), may hold values 0 or 1
Outputs:
- maxima: float32 [4, 256], P(None, ('section', 'shard'))
Inputs may be any that keep to these rules, and one draw needn't show every extreme that they name: `kept_slab`: every row has unit Euclidean length up to bfloat16 rounding. `new_rows`: every row has unit Euclidean length up to bfloat16 rounding.
All inputs are finite; a program needn't handle non-finite values. No bound on the sum of `append_mask` on one device may be relied on, other than what follows from the above.
Results may differ from a plain program's by a relative error of at most 0.0003.
Values may be sent and summed in bfloat16 or wider, within the bound.
No kernel may reach another device: no remote copies, remote signals or barrier semaphores. Data moves between devices by JAX's collectives and lax.ppermute only.
A program may use at most 64 MiB of HBM per device.

v0:
```python
import jax
import jax.numpy as jnp
from jax import lax
from jax.sharding import PartitionSpec as P


def per_device(kept_slab, new_rows, append_mask):
    micro_count = new_rows.shape[0]
    own_count = new_rows.shape[1]
    width = new_rows.shape[2]
    devices_total = lax.axis_size("section") * lax.axis_size("shard")
    batch_rows = own_count * devices_total
    append_flags = append_mask.astype(jnp.bfloat16)
    gathered_rows, gathered_flags = (
        lax.all_gather(new_rows, ("section", "shard"), axis=1, tiled=True),
        lax.all_gather(append_flags, ("section", "shard"), axis=1, tiled=True),
    )
    flattened = gathered_rows.reshape(micro_count * batch_rows, width)
    slab_rows = kept_slab.shape[0]
    block_rows = min(512, slab_rows)
    kept_blocks = kept_slab.reshape(slab_rows // block_rows, block_rows, width)

    def visit(highest, block):
        scores = lax.dot_general(
            flattened, block, (((1,), (1,)), ((), ())), preferred_element_type=jnp.float32
        )
        return (jnp.maximum(highest, jnp.max(scores, axis=1)), None)

    slab_flat, _ = lax.scan(
        visit, jnp.full((micro_count * batch_rows,), -3.0, jnp.float32), kept_blocks
    )
    slab_state = slab_flat.reshape(micro_count, batch_rows)
    later = lax.broadcasted_iota(
        jnp.int32, (micro_count, 1, micro_count, 1), 0
    ) > lax.broadcasted_iota(jnp.int32, (micro_count, 1, micro_count, 1), 2)
    cross = jnp.einsum("qid,kjd->qikj", new_rows, gathered_rows, preferred_element_type=jnp.float32)
    usable = later & (gathered_flags[None, None, :, :] > 0.5)
    stream_state = jnp.max(jnp.where(usable, cross, jnp.float32(-3.0)), axis=(2, 3))
    received = lax.all_to_all(
        slab_state, ("section", "shard"), split_axis=1, concat_axis=0, tiled=True
    )
    own_slab = jnp.max(received.reshape(devices_total, micro_count, own_count), axis=0)
    return jnp.maximum(own_slab, stream_state)


def solution(mesh):
    return jax.shard_map(
        per_device,
        mesh=mesh,
        in_specs=(
            P(("section", "shard"), None),
            P(None, ("section", "shard"), None),
            P(None, ("section", "shard")),
        ),
        out_specs=P(None, ("section", "shard")),
        check_vma=False,
    )
```

profile of v0, /device:TPU:0, one launch (start us, length us, event | category | flops | bytes accessed | tf_op | source)
XLA Modules:
  0.0 118.4 jit_solution(1405508363463907266)
XLA Ops:
  6.5 0.0 all-gather.3.cloned.1.call-start
  6.5 0.7 all-gather.3.cloned.1.call-update
  7.3 0.7 convert_bitcast_fusion
  8.0 70.0 %all-gather = bf16[32,8,4]{1,2,0:T(4,128)(2,1)S(1)} all-gather(bf16[1,8,4]{1,2,0:T(4,128)(2,1)S(1)} %convert_bitcast_fusion), channel_id=1, replica_groups=mesh['section'=8,'shard'=4] {'section','shard'}, dimensions={0}, use_global_device_ids=true | all-gather | bytes 2112 | tf_op jit(solution)/shard_map/all_gather | solution.py:16
  78.0 0.1 copy.8
  78.1 0.1 copy.9
  78.2 0.1 reshape.34
  78.3 0.1 broadcast_and_fusion
  78.4 0.0 all-gather.3.cloned.1.call-done
  78.4 0.0 copy-start
  78.4 21.7 %while.11 = (s32[]{:T(128)}, f32[1024]{0:T(1024)S(1)}, bf16[8,512,768]{2,1,0:T(8,128)(2,1)}, bf16[1024,768]{1,0:T(8,128)(2,1)}, s32[]{:T(128)}, /*index=5*/s32[]{:T(128)}) while((s32[]{:T(128)}, f32[1024]{0:T(1024)S(1)}, bf16[8,512,768]{2,1,0:T(8,128)(2,1)}, bf16[1024,768]{1,0:T(8,128)(2,1)}, s32[]{:T(128)}, ...), condition=%wide.region_2.3_spmd.clone, body=%wide.region_0.2_spmd.clone.sunk | while | flops 805831680 | bytes 2375771 | solution.py:29
  78.4 2.7 %convolution_reduce_fusion.2 = f32[1024]{0:T(1024)S(1)} fusion(bf16[1024,768]{1,0:T(8,128)(2,1)} %get-tuple-element.91, bf16[8,512,768]{2,1,0:T(8,128)(2,1)} %get-tuple-element.90, s32[]{:T(128)S(6)} %copy.13), kind=kOutput, calls=%fused_computation.clone.1 | convolution fusion | flops 805829632 | bytes 2363396 | tf_op jit(solution)/shard_map/while/body/eval_jaxpr/dot_general | solution.py:24
  81.1 2.7 %convolution_reduce_fusion.2 = f32[1024]{0:T(1024)S(1)} fusion(bf16[1024,768]{1,0:T(8,128)(2,1)} %get-tuple-element.91, bf16[8,512,768]{2,1,0:T(8,128)(2,1)} %get-tuple-element.90, s32[]{:T(128)S(6)} %copy.13), kind=kOutput, calls=%fused_computation.clone.1 | convolution fusion | flops 805829632 | bytes 2363396 | tf_op jit(solution)/shard_map/while/body/eval_jaxpr/dot_general | solution.py:24
  83.9 2.7 %convolution_reduce_fusion.2 = f32[1024]{0:T(1024)S(1)} fusion(bf16[1024,768]{1,0:T(8,128)(2,1)} %get-tuple-element.91, bf16[8,512,768]{2,1,0:T(8,128)(2,1)} %get-tuple-element.90, s32[]{:T(128)S(6)} %copy.13), kind=kOutput, calls=%fused_computation.clone.1 | convolution fusion | flops 805829632 | bytes 2363396 | tf_op jit(solution)/shard_map/while/body/eval_jaxpr/dot_general | solution.py:24
  86.6 2.7 %convolution_reduce_fusion.2 = f32[1024]{0:T(1024)S(1)} fusion(bf16[1024,768]{1,0:T(8,128)(2,1)} %get-tuple-element.91, bf16[8,512,768]{2,1,0:T(8,128)(2,1)} %get-tuple-element.90, s32[]{:T(128)S(6)} %copy.13), kind=kOutput, calls=%fused_computation.clone.1 | convolution fusion | flops 805829632 | bytes 2363396 | tf_op jit(solution)/shard_map/while/body/eval_jaxpr/dot_general | solution.py:24
  89.3 2.7 %convolution_reduce_fusion.2 = f32[1024]{0:T(1024)S(1)} fusion(bf16[1024,768]{1,0:T(8,128)(2,1)} %get-tuple-element.91, bf16[8,512,768]{2,1,0:T(8,128)(2,1)} %get-tuple-element.90, s32[]{:T(128)S(6)} %copy.13), kind=kOutput, calls=%fused_computation.clone.1 | convolution fusion | flops 805829632 | bytes 2363396 | tf_op jit(solution)/shard_map/while/body/eval_jaxpr/dot_general | solution.py:24
  92.0 2.7 %convolution_reduce_fusion.2 = f32[1024]{0:T(1024)S(1)} fusion(bf16[1024,768]{1,0:T(8,128)(2,1)} %get-tuple-element.91, bf16[8,512,768]{2,1,0:T(8,128)(2,1)} %get-tuple-element.90, s32[]{:T(128)S(6)} %copy.13), kind=kOutput, calls=%fused_computation.clone.1 | convolution fusion | flops 805829632 | bytes 2363396 | tf_op jit(solution)/shard_map/while/body/eval_jaxpr/dot_general | solution.py:24
  94.7 2.7 %convolution_reduce_fusion.2 = f32[1024]{0:T(1024)S(1)} fusion(bf16[1024,768]{1,0:T(8,128)(2,1)} %get-tuple-element.91, bf16[8,512,768]{2,1,0:T(8,128)(2,1)} %get-tuple-element.90, s32[]{:T(128)S(6)} %copy.13), kind=kOutput, calls=%fused_computation.clone.1 | convolution fusion | flops 805829632 | bytes 2363396 | tf_op jit(solution)/shard_map/while/body/eval_jaxpr/dot_general | solution.py:24
  97.4 2.7 %convolution_reduce_fusion.2 = f32[1024]{0:T(1024)S(1)} fusion(bf16[1024,768]{1,0:T(8,128)(2,1)} %get-tuple-element.91, bf16[8,512,768]{2,1,0:T(8,128)(2,1)} %get-tuple-element.90, s32[]{:T(128)S(6)} %copy.13), kind=kOutput, calls=%fused_computation.clone.1 | convolution fusion | flops 805829632 | bytes 2363396 | tf_op jit(solution)/shard_map/while/body/eval_jaxpr/dot_general | solution.py:24
  100.1 0.1 all_to_all.10
  100.2 0.7 copy.7
  100.9 2.5 %all-to-all-start = ((f32[4,32,8]{2,0,1:T(4,128)}), f32[4,32,8]{2,0,1:T(4,128)S(1)}, u32[]{:S(2)}, u32[]{:S(2)}) async-start(f32[4,32,8]{2,0,1:T(4,128)} %copy.7), calls=%async_computation | async-start | bytes 131072 | tf_op jit(solution)/shard_map/all_to_all | solution.py:39
  103.4 0.0 copy-done
  103.4 2.1 %fusion.8 = f32[4,8]{1,0:T(4,128)S(1)} fusion(bf16[4,256,768]{2,1,0:T(8,128)(2,1)} %bitcast.30, pred[4,4,256]{2,1,0:T(4,128)(4,1)S(1)} %broadcast_and_fusion, bf16[4,8,768]{2,1,0:T(8,128)(2,1)S(1)} %copy-done), kind=kOutput, calls=%fused_computation.8 | convolution fusion | flops 50397152 | bytes 1626240 | tf_op jit(solution)/shard_map/qid,kjd->qikj/dot_general | solution.py:36
  105.5 5.4 %all-to-all-done = f32[4,32,8]{2,0,1:T(4,128)S(1)} async-done(((f32[4,32,8]{2,0,1:T(4,128)}), f32[4,32,8]{2,0,1:T(4,128)S(1)}, u32[]{:S(2)}, u32[]{:S(2)}) %all-to-all-start) | async-done | bytes 4128 | tf_op jit(solution)/shard_map/all_to_all | solution.py:39
  111.0 0.6 max.6
  (12 shorter events, 0.1 us)
Async XLA Ops:
  6.5 71.9 %all-gather.3.cloned.1.call-start = ((), (), s32[]{:S(2)}) async-start(), calls=%async_computation.1 | async-start | bytes 1622016 | tf_op jit(solution)/shard_map/all_gather | solution.py:15
  78.4 25.0 %copy-start = (bf16[4,8,768]{2,1,0:T(8,128)(2,1)S(1)}, bf16[4,8,768]{2,1,0:T(8,128)(2,1)}, u32[]{:S(2)}) copy-start(bf16[4,8,768]{2,1,0:T(8,128)(2,1)} %param.6) | copy-start | bytes 147460
  100.9 10.1 %all-to-all-start = ((f32[4,32,8]{2,0,1:T(4,128)}), f32[4,32,8]{2,0,1:T(4,128)S(1)}, u32[]{:S(2)}, u32[]{:S(2)}) async-start(f32[4,32,8]{2,0,1:T(4,128)} %copy.7), calls=%async_computation | async-start | bytes 131072 | tf_op jit(solution)/shard_map/all_to_all | solution.py:39
Sparse Core Ops, SparseCore 0:
  10.2 55.3 all-gather.2
where the time goes:
time: 119 us; the launch traced here: 118 us
  blocking collectives  70 us (59%)
  matrix products  23.5 us (20%)
  between operations  13.5 us (11%)
  waiting for transfers between devices  6.15 us (5%)
  starting transfers between devices  2.55 us (2%)
  other arithmetic  1.46 us (1%)
    all_gather x1, blocking collectives, per_device(): lax.all_gather(append_flags, ('section', 'shard'), axis=1, tiled=True)  70 us
    dot_general x8, matrix products, visit(): lax.dot_general(flattened, block, (((1,), (1,)), ((), ())), preferred_ele...  21.4 us
    all_to_all x1, waiting for transfers between devices, per_device(): lax.all_to_all(slab_state, ('section', 'shard'), split_axis=1, concat_axi...  5.44 us
    all_to_all x1, starting transfers between devices, per_device(): lax.all_to_all(slab_state, ('section', 'shard'), split_axis=1, concat_axi...  2.55 us
  transfers between devices with their start and end apart: 2, of which 1 were waited for; matrix products, arithmetic and copies ran while one was open for 3% of the time, Pallas kernels for 0%

commit v1 on v0

--- a/solution.py
+++ b/solution.py
@@ -36,9 +36,10 @@
     cross = jnp.einsum("qid,kjd->qikj", new_rows, gathered_rows, preferred_element_type=jnp.float32)
     usable = later & (gathered_flags[None, None, :, :] > 0.5)
     stream_state = jnp.max(jnp.where(usable, cross, jnp.float32(-3.0)), axis=(2, 3))
-    received = lax.all_to_all(
-        slab_state, ("section", "shard"), split_axis=1, concat_axis=0, tiled=True
-    )
+    n_dev = lax.axis_size(("section", "shard"))
+    pieces = jnp.stack(jnp.split(slab_state, n_dev, axis=1), axis=0)
+    pieces = lax.all_to_all(pieces, ("section", "shard"), split_axis=0, concat_axis=0)
+    received = jnp.concatenate(pieces, axis=0)
     own_slab = jnp.max(received.reshape(devices_total, micro_count, own_count), axis=0)
     return jnp.maximum(own_slab, stream_state)
 

time: 119 us -> 139 us (1.17)
  local copies, waits for them, and re-layouts: 1.05 us -> 21 us
    unnamed x2 -> x33, local copies, waits for them, and re-layouts: 0.01 us -> 20.1 us
  transfers between devices with their start and end apart: 2 -> 2, of which waited for: 1 -> 1; matrix products, arithmetic and copies ran while one was open for 3% -> 2% of each run, Pallas kernels for 0% -> 0%
where the time goes in v1:
time: 139 us; the launch traced here: 138 us
  blocking collectives  70 us (50%)
  matrix products  23.4 us (17%)
  local copies, waits for them, and re-layouts  21 us (15%)
  between operations  13.5 us (10%)
  waiting for transfers between devices  6.15 us (4%)
  starting transfers between devices  2.55 us (2%)
  other arithmetic  1.46 us (1%)
    all_gather x1, blocking collectives, per_device(): lax.all_gather(append_flags, ('section', 'shard'), axis=1, tiled=True)  70 us
    dot_general x8, matrix products, visit(): lax.dot_general(flattened, block, (((1,), (1,)), ((), ())), preferred_ele...  21.4 us
    unnamed x33, local copies, waits for them, and re-layouts  20.1 us
    all_to_all x1, waiting for transfers between devices, per_device(): lax.all_to_all(pieces, ('section', 'shard'), split_axis=0, concat_axis=0)  5.44 us
  transfers between devices with their start and end apart: 2, of which 1 were waited for; matrix products, arithmetic and copies ran while one was open for 2% of the time, Pallas kernels for 0%

profile of v1, /device:TPU:0, one launch (start us, length us, event | category | flops | bytes accessed | tf_op | source)
XLA Modules:
  0.0 138.4 jit_solution(10985815510101138703)
XLA Ops:
  6.5 0.0 all-gather.3.cloned.1.call-start
  6.5 0.7 all-gather.3.cloned.1.call-update
  7.3 0.7 convert_bitcast_fusion
  8.0 70.0 %all-gather = bf16[32,8,4]{1,2,0:T(4,128)(2,1)S(1)} all-gather(bf16[1,8,4]{1,2,0:T(4,128)(2,1)S(1)} %convert_bitcast_fusion), channel_id=1, replica_groups=mesh['section'=8,'shard'=4] {'section','shard'}, dimensions={0}, use_global_device_ids=true | all-gather | bytes 2112 | tf_op jit(solution)/shard_map/all_gather | solution.py:16
  78.0 0.1 copy.73
  78.1 0.1 copy.74
  78.2 0.1 reshape.31
  78.3 0.1 broadcast_and_fusion
  78.4 0.0 all-gather.3.cloned.1.call-done
  78.4 0.0 copy-start
  78.4 21.7 %while.11 = (s32[]{:T(128)}, f32[1024]{0:T(1024)S(1)}, bf16[8,512,768]{2,1,0:T(8,128)(2,1)}, bf16[1024,768]{1,0:T(8,128)(2,1)}, s32[]{:T(128)}, /*index=5*/s32[]{:T(128)}) while((s32[]{:T(128)}, f32[1024]{0:T(1024)S(1)}, bf16[8,512,768]{2,1,0:T(8,128)(2,1)}, bf16[1024,768]{1,0:T(8,128)(2,1)}, s32[]{:T(128)}, ...), condition=%wide.region_2.3_spmd.clone, body=%wide.region_0.2_spmd.clone.sunk | while | flops 805831680 | bytes 2375771 | solution.py:29
  78.4 2.7 %convolution_reduce_fusion.2 = f32[1024]{0:T(1024)S(1)} fusion(bf16[1024,768]{1,0:T(8,128)(2,1)} %get-tuple-element.91, bf16[8,512,768]{2,1,0:T(8,128)(2,1)} %get-tuple-element.90, s32[]{:T(128)S(6)} %copy.78), kind=kOutput, calls=%fused_computation.clone.1 | convolution fusion | flops 805829632 | bytes 2363396 | tf_op jit(solution)/shard_map/while/body/eval_jaxpr/dot_general | solution.py:24
  81.1 2.7 %convolution_reduce_fusion.2 = f32[1024]{0:T(1024)S(1)} fusion(bf16[1024,768]{1,0:T(8,128)(2,1)} %get-tuple-element.91, bf16[8,512,768]{2,1,0:T(8,128)(2,1)} %get-tuple-element.90, s32[]{:T(128)S(6)} %copy.78), kind=kOutput, calls=%fused_computation.clone.1 | convolution fusion | flops 805829632 | bytes 2363396 | tf_op jit(solution)/shard_map/while/body/eval_jaxpr/dot_general | solution.py:24
  83.9 2.7 %convolution_reduce_fusion.2 = f32[1024]{0:T(1024)S(1)} fusion(bf16[1024,768]{1,0:T(8,128)(2,1)} %get-tuple-element.91, bf16[8,512,768]{2,1,0:T(8,128)(2,1)} %get-tuple-element.90, s32[]{:T(128)S(6)} %copy.78), kind=kOutput, calls=%fused_computation.clone.1 | convolution fusion | flops 805829632 | bytes 2363396 | tf_op jit(solution)/shard_map/while/body/eval_jaxpr/dot_general | solution.py:24
  86.6 2.7 %convolution_reduce_fusion.2 = f32[1024]{0:T(1024)S(1)} fusion(bf16[1024,768]{1,0:T(8,128)(2,1)} %get-tuple-element.91, bf16[8,512,768]{2,1,0:T(8,128)(2,1)} %get-tuple-element.90, s32[]{:T(128)S(6)} %copy.78), kind=kOutput, calls=%fused_computation.clone.1 | convolution fusion | flops 805829632 | bytes 2363396 | tf_op jit(solution)/shard_map/while/body/eval_jaxpr/dot_general | solution.py:24
  89.3 2.7 %convolution_reduce_fusion.2 = f32[1024]{0:T(1024)S(1)} fusion(bf16[1024,768]{1,0:T(8,128)(2,1)} %get-tuple-element.91, bf16[8,512,768]{2,1,0:T(8,128)(2,1)} %get-tuple-element.90, s32[]{:T(128)S(6)} %copy.78), kind=kOutput, calls=%fused_computation.clone.1 | convolution fusion | flops 805829632 | bytes 2363396 | tf_op jit(solution)/shard_map/while/body/eval_jaxpr/dot_general | solution.py:24
  92.0 2.7 %convolution_reduce_fusion.2 = f32[1024]{0:T(1024)S(1)} fusion(bf16[1024,768]{1,0:T(8,128)(2,1)} %get-tuple-element.91, bf16[8,512,768]{2,1,0:T(8,128)(2,1)} %get-tuple-element.90, s32[]{:T(128)S(6)} %copy.78), kind=kOutput, calls=%fused_computation.clone.1 | convolution fusion | flops 805829632 | bytes 2363396 | tf_op jit(solution)/shard_map/while/body/eval_jaxpr/dot_general | solution.py:24
  94.7 2.7 %convolution_reduce_fusion.2 = f32[1024]{0:T(1024)S(1)} fusion(bf16[1024,768]{1,0:T(8,128)(2,1)} %get-tuple-element.91, bf16[8,512,768]{2,1,0:T(8,128)(2,1)} %get-tuple-element.90, s32[]{:T(128)S(6)} %copy.78), kind=kOutput, calls=%fused_computation.clone.1 | convolution fusion | flops 805829632 | bytes 2363396 | tf_op jit(solution)/shard_map/while/body/eval_jaxpr/dot_general | solution.py:24
  97.4 2.7 %convolution_reduce_fusion.2 = f32[1024]{0:T(1024)S(1)} fusion(bf16[1024,768]{1,0:T(8,128)(2,1)} %get-tuple-element.91, bf16[8,512,768]{2,1,0:T(8,128)(2,1)} %get-tuple-element.90, s32[]{:T(128)S(6)} %copy.78), kind=kOutput, calls=%fused_computation.clone.1 | convolution fusion | flops 805829632 | bytes 2363396 | tf_op jit(solution)/shard_map/while/body/eval_jaxpr/dot_general | solution.py:24
  100.1 0.6 constant_dynamic-update-slice_fusion.31
  100.7 0.7 constant_dynamic-update-slice_fusion.30
  101.4 0.6 constant_dynamic-update-slice_fusion.29
  102.0 0.7 constant_dynamic-update-slice_fusion.28
  102.7 0.7 constant_dynamic-update-slice_fusion.27
  103.3 0.6 constant_dynamic-update-slice_fusion.26
  104.0 0.7 constant_dynamic-update-slice_fusion.25
  104.7 0.6 constant_dynamic-update-slice_fusion.24
  105.3 0.6 constant_dynamic-update-slice_fusion.23
  105.9 0.7 constant_dynamic-update-slice_fusion.22
  106.6 0.6 constant_dynamic-update-slice_fusion.21
  107.3 0.7 constant_dynamic-update-slice_fusion.20
  107.9 0.7 constant_dynamic-update-slice_fusion.19
  108.6 0.6 constant_dynamic-update-slice_fusion.18
  109.2 0.7 constant_dynamic-update-slice_fusion.17
  109.9 0.6 constant_dynamic-update-slice_fusion.16
  110.5 0.6 constant_dynamic-update-slice_fusion.15
  111.1 0.7 constant_dynamic-update-slice_fusion.14
  111.7 0.6 constant_dynamic-update-slice_fusion.13
  112.4 0.7 constant_dynamic-update-slice_fusion.12
  113.0 0.7 constant_dynamic-update-slice_fusion.11
  113.7 0.6 constant_dynamic-update-slice_fusion.10
  114.3 0.7 constant_dynamic-update-slice_fusion.9
  115.0 0.6 constant_dynamic-update-slice_fusion.8
  115.6 0.6 constant_dynamic-update-slice_fusion.7
  116.3 0.7 constant_dynamic-update-slice_fusion.6
  117.0 0.6 constant_dynamic-update-slice_fusion.5
  117.6 0.7 constant_dynamic-update-slice_fusion.4
  118.3 0.7 constant_dynamic-update-slice_fusion.3
  118.9 0.6 constant_dynamic-update-slice_fusion.2
  119.6 0.7 constant_dynamic-update-slice_fusion.1
  120.2 0.6 constant_dynamic-update-slice_fusion
  120.9 2.5 %all-to-all-start = ((f32[32,4,8]{2,1,0:T(4,128)}), f32[32,4,8]{2,1,0:T(4,128)S(1)}, u32[]{:S(2)}, u32[]{:S(2)}) async-start(f32[32,4,8]{2,1,0:T(4,128)} %constant_dynamic-update-slice_fusion), calls=%async_computation | async-start | bytes 131072 | tf_op jit(solution)/shard_map/all_to_all | solution.py:41
  123.4 0.0 copy-done
  123.4 2.0 %fusion.8 = f32[4,8]{1,0:T(4,128)S(1)} fusion(bf16[4,256,768]{2,1,0:T(8,128)(2,1)} %bitcast.158, pred[4,4,256]{2,1,0:T(4,128)(4,1)S(1)} %broadcast_and_fusion, bf16[4,8,768]{2,1,0:T(8,128)(2,1)S(1)} %copy-done), kind=kOutput, calls=%fused_computation.8 | convolution fusion | flops 50397152 | bytes 1626240 | tf_op jit(solution)/shard_map/qid,kjd->qikj/dot_general | solution.py:36
  125.5 5.4 %all-to-all-done = f32[32,4,8]{2,1,0:T(4,128)S(1)} async-done(((f32[32,4,8]{2,1,0:T(4,128)}), f32[32,4,8]{2,1,0:T(4,128)S(1)}, u32[]{:S(2)}, u32[]{:S(2)}) %all-to-all-start) | async-done | bytes 4128 | tf_op jit(solution)/shard_map/all_to_all | solution.py:41
  131.0 0.6 max.6
  (13 shorter events, 0.1 us)
Async XLA Ops:
  6.5 71.9 %all-gather.3.cloned.1.call-start = ((), (), s32[]{:S(2)}) async-start(), calls=%async_computation.1 | async-start | bytes 1622016 | tf_op jit(solution)/shard_map/all_gather | solution.py:15
  78.4 45.0 %copy-start = (bf16[4,8,768]{2,1,0:T(8,128)(2,1)S(1)}, bf16[4,8,768]{2,1,0:T(8,128)(2,1)}, u32[]{:S(2)}) copy-start(bf16[4,8,768]{2,1,0:T(8,128)(2,1)} %param.6) | copy-start | bytes 147460
  120.9 10.1 %all-to-all-start = ((f32[32,4,8]{2,1,0:T(4,128)}), f32[32,4,8]{2,1,0:T(4,128)S(1)}, u32[]{:S(2)}, u32[]{:S(2)}) async-start(f32[32,4,8]{2,1,0:T(4,128)} %constant_dynamic-update-slice_fusion), calls=%async_computation | async-start | bytes 131072 | tf_op jit(solution)/shard_map/all_to_all | solution.py:41
Sparse Core Ops, SparseCore 0:
  10.2 55.3 all-gather.2
